TPU v7x, 512 devices: a whole 4x8x8 slice. The times are simulated.
512 devices in a mesh: ctx: 32 (over z_hi, y, core), tp: 16 (over x, z_lo).
Axes of the slice: x: 4, y: 8, z: 8 (z_hi: 2, z_lo: 4; z = z_hi * 4 + z_lo), core: 2. Of those that a mesh axis runs over, the one named last changes fastest.
Arguments:
- residual: bfloat16 [4352, 8192], P('ctx', 'tp'), may hold values from -64 to 64
- gate_first: bfloat16 [4352, 8192], P('ctx', 'tp'), may hold values from -6 to 6
- gate_second: bfloat16 [4352, 8192], P('ctx', 'tp'), may hold values from -6 to 6
- hyena_value: bfloat16 [4352, 8192], P('ctx', 'tp'), may hold values from -6 to 6
- short_taps: float32 [3, 3, 8192], P(None, None, 'tp'), may hold values from -3.5 to 3.5
- long_taps: bfloat16 [128, 8192], P(None, 'tp'), may hold values from -0.5 to 0.5
- norm_gain: float32 [8192], P('tp'), may hold values from 0.1 to 1.9
- queries: bfloat16 [4352, 8192], P('ctx', 'tp'), may hold values from -8 to 8
- attn_keys: bfloat16 [4352, 8192], P('ctx', 'tp'), may hold values from -8 to 8
Outputs:
- stream: bfloat16 [4352, 8192], P('ctx', 'tp')
- attended: bfloat16 [4352, 8192], P('ctx', 'tp')
All inputs are finite; a program needn't handle non-finite values.
Results may differ from a plain program's by a relative error of at most 0.007.
Values may be sent and summed in bfloat16 or wider, within the bound.
No kernel may reach another device: no remote copies, remote signals or barrier semaphores. Data moves between devices by JAX's collectives and lax.ppermute only.
A program may use at most 64 MiB of HBM per device.

v0:
```python
import math
import jax
import jax.numpy as jnp
from jax import lax
from jax.sharding import PartitionSpec as P

HD = 128


def shifted(value, axis, steps):
    count = lax.axis_size(axis)
    first, last = (max(0, -steps), min(count, count - steps))
    return lax.ppermute(value, axis, [(source, source + steps) for source in range(first, last)])


def featurize(extended, tap_weights, count):
    taps_total = tap_weights.shape[0]
    result = jnp.zeros((count, extended.shape[1]), jnp.float32)
    for lag_index in range(taps_total):
        begin = taps_total - 1 - lag_index
        result = result + tap_weights[lag_index] * extended[begin : begin + count].astype(
            jnp.float32
        )
    return result


def long_filter(extended, long_taps, count):
    filter_len = long_taps.shape[0]
    padded = extended.astype(jnp.float32)
    tap_table = long_taps.astype(jnp.float32)

    def tap_group(group_index, running):
        for inner_index in range(8):
            lag_index = group_index * 8 + inner_index
            window = lax.dynamic_slice_in_dim(padded, filter_len - 1 - lag_index, count, 0)
            running = (
                running + lax.dynamic_index_in_dim(tap_table, lag_index, 0, keepdims=False) * window
            )
        return running

    return lax.fori_loop(
        0, filter_len // 8, tap_group, jnp.zeros((count, extended.shape[1]), jnp.float32)
    )


def shards(
    residual,
    gate_first,
    gate_second,
    hyena_value,
    short_taps,
    long_taps,
    norm_gain,
    queries,
    attn_keys,
):
    rows = residual.shape[0]
    chans = residual.shape[1]
    filter_len = long_taps.shape[0]
    reach = short_taps.shape[1]
    prev_first, prev_second, prev_value = shifted(
        (
            gate_first[rows - reach + 1 :],
            gate_second[rows - reach + 1 :],
            hyena_value[rows - reach + 1 :],
        ),
        "ctx",
        1,
    )
    feat_first = featurize(jnp.concatenate([prev_first, gate_first], axis=0), short_taps[0], rows)
    feat_second = featurize(
        jnp.concatenate([prev_second, gate_second], axis=0), short_taps[1], rows
    )
    feat_value = featurize(jnp.concatenate([prev_value, hyena_value], axis=0), short_taps[2], rows)
    product = (feat_first * feat_value).astype(jnp.bfloat16)
    prev_product = shifted(product[rows - filter_len + 1 :], "ctx", 1)
    extended = jnp.concatenate([prev_product, product], axis=0)
    filtered = long_filter(extended, long_taps, rows)
    stream = (residual.astype(jnp.float32) + feat_second * filtered).astype(jnp.bfloat16)
    stream_f = stream.astype(jnp.float32)
    row_squares = jnp.sum(stream_f * stream_f, axis=1)
    row_totals = lax.psum(row_squares, "tp")
    inverse = 1.0 / jnp.sqrt(row_totals / (chans * lax.axis_size("tp")) + 1e-06)
    heads = chans // HD
    scale = 1.0 / math.sqrt(HD)
    my_index = lax.axis_index("ctx")
    query_pos = my_index * rows + jnp.arange(rows)
    last_query = my_index * rows + rows - 1
    query_heads = queries.reshape(rows, heads, HD)
    init_state = (
        jnp.full((heads, rows), -1e30, jnp.float32),
        jnp.zeros((heads, rows), jnp.float32),
        jnp.zeros((rows, heads, HD), jnp.float32),
    )
    values = (stream_f * inverse[:, None] * norm_gain).astype(jnp.bfloat16)
    key_piece = lax.all_gather(attn_keys, "ctx", axis=0, tiled=True)
    raw_piece = lax.all_gather(values, "ctx", axis=0, tiled=True)
    piece_rows = key_piece.shape[0]
    block = math.gcd(piece_rows, 1536)

    def block_step(block_index, state):
        offset = block_index * block
        key_block = lax.dynamic_slice_in_dim(key_piece, offset, block, 0)
        raw_block = lax.dynamic_slice_in_dim(raw_piece, offset, block, 0)

        def update(current):
            running_max, running_sum, accum = current
            scores = (
                jnp.einsum(
                    "shd,phd->hsp",
                    query_heads,
                    key_block.reshape(block, heads, HD),
                    preferred_element_type=jnp.float32,
                )
                * scale
            )
            key_pos = offset + jnp.arange(block)
            allowed = (key_pos[None, :] <= query_pos[:, None])[None]
            masked = jnp.where(allowed, scores, -1e30)
            new_max = jnp.maximum(running_max, jnp.max(masked, axis=2))
            factor = jnp.exp(running_max - new_max)
            expo = jnp.where(allowed, jnp.exp(scores - new_max[:, :, None]), 0.0)
            new_sum = running_sum * factor + jnp.sum(expo, axis=2)
            weights = expo.astype(jnp.bfloat16)
            contrib = jnp.einsum(
                "hsp,phd->shd",
                weights,
                raw_block.reshape(block, heads, HD),
                preferred_element_type=jnp.float32,
            )
            new_accum = accum * factor.T[:, :, None] + contrib
            return (new_max, new_sum, new_accum)

        def keep_state(current):
            return current

        return lax.cond(offset <= last_query, update, keep_state, state)

    final_state = lax.fori_loop(0, piece_rows // block, block_step, init_state)
    running_sum = final_state[1]
    accum = final_state[2]
    attended = (accum / running_sum.T[:, :, None]).reshape(rows, chans).astype(jnp.bfloat16)
    return (stream, attended)


def solution(mesh):
    placed = (
        P("ctx", "tp"),
        P("ctx", "tp"),
        P("ctx", "tp"),
        P("ctx", "tp"),
        P(None, None, "tp"),
        P(None, "tp"),
        P("tp"),
        P("ctx", "tp"),
        P("ctx", "tp"),
    )
    return jax.shard_map(
        shards,
        mesh=mesh,
        in_specs=placed,
        out_specs=(P("ctx", "tp"), P("ctx", "tp")),
        check_vma=False,
    )
```

profile of v0, /device:TPU:443, one launch (start us, length us, event | category | flops | bytes accessed | tf_op | source)
XLA Modules:
  0.0 276.9 jit_solution(2932315413179396833)
XLA Ops:
  8.7 1.3 collective-permute-start.1
  10.7 1.3 collective-permute-start.2
  12.8 1.7 collective-permute-done.2
  14.5 1.5 multiply_convert_fusion
  16.0 1.3 collective-permute-start.3
  18.0 1.3 collective-permute-start
  19.3 0.9 convert_element_type.71
  21.2 8.7 %while.36 = (s32[]{:T(128)}, f32[136,512]{1,0:T(8,128)S(1)}, f32[128,512]{1,0:T(8,128)S(1)}, f32[263,512]{1,0:T(8,128)S(1)}, s32[]{:T(128)}, /*index=5*/s32[]{:T...) while((s32[]{:T(128)}, f32[136,512]{1,0:T(8,128)S(1)}, ...), condition=%wide.region_1.2_spmd.clone, body=%wide.region_0.1_spmd.clone.sunk | while | flops 1183811 | bytes 2835447 | solution.py:41
  30.1 25.8 %psum.7 = f32[136]{0:T(256)S(1)} all-reduce(f32[136]{0:T(256)S(1)} %get-tuple-element.512), channel_id=1, replica_groups=mesh['ctx'=32,'tp'=16] {'tp'}, use_global_device_ids=true, to_apply=%region_3.4 | all-reduce | flops 136 | bytes 1088 | tf_op jit(solution)/shard_map/psum | solution.py:82
  56.8 58.0 %all-gather.3.cloned.1.call-done = bf16[4352,512]{1,0:T(8,128)(2,1)} async-done(((bf16[136,512]{1,0:T(8,128)(2,1)}), bf16[4352,512]{1,0:T(8,128)(2,1)}) %all-gather.3.cloned.1.call-update) | async-done | bytes 4456464 | tf_op jit(solution)/shard_map/all_gather | solution.py:96
  114.8 6.4 %copy.20 = bf16[4352,512]{0,1:T(8,128)(2,1)} copy(bf16[4352,512]{1,0:T(8,128)(2,1)} %all-gather.3.cloned.1.call-done) | data formatting | bytes 8912896
  121.2 100.1 %all-gather.5.cloned.1.call-done = bf16[4352,512]{1,0:T(8,128)(2,1)} async-done(((bf16[136,512]{1,0:T(8,128)(2,1)}), bf16[4352,512]{1,0:T(8,128)(2,1)}) %all-gather.5.cloned.1.call-update) | async-done | bytes 4456464 | tf_op jit(solution)/shard_map/all_gather | solution.py:97
  221.4 6.6 %copy.22 = bf16[4352,512]{0,1:T(8,128)(2,1)} copy(bf16[4352,512]{1,0:T(8,128)(2,1)} %all-gather.5.cloned.1.call-done) | data formatting | bytes 8912896
  228.0 41.2 %while.35 = (s32[]{:T(128)}, f32[4,136]{1,0:T(4,128)S(1)}, f32[4,136]{1,0:T(4,128)S(1)}, f32[136,4,128]{2,0,1:T(8,128)S(1)}, s32[]{:T(128)}, /*index=5*/bf16[435...) while((s32[]{:T(128)}, f32[4,136]{1,0:T(4,128)S(1)}, ...), condition=%wide.region_9.10_spmd.clone, body=%wide.region_4.9_spmd.clone.sunk | while | flops 72732656 | bytes 4118965 | solution.py:139
  228.0 2.4 conditional.3
  228.0 1.1 constant_dynamic-slice_fusion
  230.4 2.4 conditional.3
  230.5 1.1 constant_dynamic-slice_fusion
  232.9 2.4 conditional.3
  232.9 1.1 constant_dynamic-slice_fusion
  235.3 2.4 conditional.3
  235.3 1.1 constant_dynamic-slice_fusion
  237.7 2.4 conditional.3
  237.7 1.1 constant_dynamic-slice_fusion
  240.1 2.4 conditional.3
  240.2 1.1 constant_dynamic-slice_fusion
  242.6 2.4 conditional.3
  242.6 1.1 constant_dynamic-slice_fusion
  245.0 2.4 conditional.3
  245.0 1.1 constant_dynamic-slice_fusion
  247.4 2.4 conditional.3
  247.4 1.1 constant_dynamic-slice_fusion
  249.8 2.4 conditional.3
  249.9 1.1 constant_dynamic-slice_fusion
  252.3 2.4 conditional.3
  252.3 1.1 constant_dynamic-slice_fusion
  254.7 2.4 conditional.3
  254.7 1.1 constant_dynamic-slice_fusion
  257.1 2.4 conditional.3
  257.1 1.1 constant_dynamic-slice_fusion
  259.5 2.4 conditional.3
  259.6 1.1 constant_dynamic-slice_fusion
  262.0 2.4 conditional.3
  262.0 1.1 constant_dynamic-slice_fusion
  264.4 2.4 conditional.3
  264.4 1.1 constant_dynamic-slice_fusion
  266.8 2.4 conditional.3
  266.8 1.1 constant_dynamic-slice_fusion
  (234 shorter events, 34.1 us)
Async XLA Ops:
  7.2 49.6 %copy-start = (bf16[136,512]{1,0:T(8,128)(2,1)S(1)}, bf16[136,512]{1,0:T(8,128)(2,1)}, u32[]{:S(2)}) copy-start(bf16[136,512]{1,0:T(8,128)(2,1)} %param.22) | copy-start | bytes 417796
  7.2 107.6 %all-gather.3.cloned.1.call-start = ((), (), s32[]{:S(2)}) async-start(), calls=%async_computation | async-start | bytes 4595712 | tf_op jit(solution)/shard_map/all_gather | solution.py:96
  7.9 213.5 %all-gather.5.cloned.1.call-start = ((), (), s32[]{:S(2)}) async-start(), calls=%async_computation.1 | async-start | bytes 4595712 | tf_op jit(solution)/shard_map/all_gather | solution.py:97
  8.7 4.2 %collective-permute-start.1 = (bf16[2,512]{1,0:T(2,128)(2,1)S(1)}, bf16[2,512]{1,0:T(2,128)(2,1)S(1)}, u32[]{:S(2)}, u32[]{:S(2)}) collective-permute-start(bf16[2,512]{1,0:T(2,128)(2,1)S(1)} %slice.86), channel_id=1, source_target_pairs={{0,16},{16,32},{32,48},{48,64},{64,80},{80,96},{96,112},{112,128},... | collective-permute-start | bytes 6152 | tf_op jit(solution)/shard_map/ppermute | solution.py:13
  10.7 3.8 %collective-permute-start.2 = (bf16[2,512]{1,0:T(2,128)(2,1)S(1)}, bf16[2,512]{1,0:T(2,128)(2,1)S(1)}, u32[]{:S(2)}, u32[]{:S(2)}) collective-permute-start(bf16[2,512]{1,0:T(2,128)(2,1)S(1)} %slice.92), channel_id=1, source_target_pairs={{0,16},{16,32},{32,48},{48,64},{64,80},{80,96},{96,112},{112,128},... | collective-permute-start | bytes 6152 | tf_op jit(solution)/shard_map/ppermute | solution.py:13
  16.0 5.1 %collective-permute-start.3 = (bf16[127,512]{1,0:T(8,128)(2,1)S(1)}, bf16[127,512]{1,0:T(8,128)(2,1)S(1)}, u32[]{:S(2)}, u32[]{:S(2)}) collective-permute-start(bf16[127,512]{1,0:T(8,128)(2,1)S(1)} %slice.103), channel_id=1, source_target_pairs={{0,16},{16,32},{32,48},{48,64},{64,80},{80,96},{96,112},{112,128},... | collective-permute-start | bytes 390152 | tf_op jit(solution)/shard_map/ppermute | solution.py:13
  18.0 11.9 %collective-permute-start = (bf16[2,512]{1,0:T(2,128)(2,1)S(1)}, bf16[2,512]{1,0:T(2,128)(2,1)S(1)}, u32[]{:S(2)}, u32[]{:S(2)}) collective-permute-start(bf16[2,512]{1,0:T(2,128)(2,1)S(1)} %slice.80), channel_id=1, source_target_pairs={{0,16},{16,32},{32,48},{48,64},{64,80},{80,96},{96,112},{112,128},... | collective-permute-start | bytes 6152 | tf_op jit(solution)/shard_map/ppermute | solution.py:13
  21.2 8.7 %copy-start.2 = (bf16[136,512]{1,0:T(8,128)(2,1)S(1)}, bf16[136,512]{1,0:T(8,128)(2,1)}, u32[]{:S(2)}) copy-start(bf16[136,512]{1,0:T(8,128)(2,1)} %param.17) | copy-start | bytes 417796
  21.2 8.7 %copy-start.3 = (bf16[136,512]{1,0:T(8,128)(2,1)S(1)}, bf16[136,512]{1,0:T(8,128)(2,1)}, u32[]{:S(2)}) copy-start(bf16[136,512]{1,0:T(8,128)(2,1)} %param.15) | copy-start | bytes 417796
  21.2 34.8 %copy-start.4 = (f32[512]{0:T(512)S(1)}, f32[512]{0:T(512)}, u32[]{:S(2)}) copy-start(f32[512]{0:T(512)} %param.21) | copy-start | bytes 6148
  30.1 91.1 %copy-start.1 = (bf16[136,512]{1,0:T(8,128)(2,1)}, bf16[136,512]{1,0:T(8,128)(2,1)S(1)}, u32[]{:S(2)}) copy-start(bf16[136,512]{1,0:T(8,128)(2,1)S(1)} %get-tuple-element.513) | copy-start | bytes 417796
Sparse Core Ops, SparseCore 0:
  11.4 103.3 all-gather.2
  118.8 102.5 all-gather.4
where the time goes:
time: 278 us; the launch traced here: 277 us
  waiting for transfers between devices  161 us (58%)
  local copies, waits for them, and re-layouts  35 us (13%)
  blocking collectives  25.8 us (9%)
  other arithmetic  18.4 us (7%)
  between operations  14.2 us (5%)
  matrix products  12.7 us (5%)
  starting transfers between devices  5.21 us (2%)
  loops' own time  4.14 us (1%)
    all_gather x1, waiting for transfers between devices, shards(): raw_piece = lax.all_gather(values, 'ctx', axis=0, tiled=True)  100 us
    all_gather x1, waiting for transfers between devices, shards(): key_piece = lax.all_gather(attn_keys, 'ctx', axis=0, tiled=True)  58 us
    psum x1, blocking collectives, shards(): row_totals = lax.psum(row_squares, 'tp')  25.8 us
    dynamic_slice x17, local copies, waits for them, and re-layouts, block_step(): raw_block = lax.dynamic_slice_in_dim(raw_piece, offset, block, 0)  18.3 us
    unnamed x13, local copies, waits for them, and re-layouts  13 us
    dot_general x17, matrix products, update(): jnp.einsum('shd,phd->hsp', query_heads, key_block.reshape(block, heads, H...  6.99 us
    reduce_sum x17, other arithmetic, update(): new_sum = running_sum * factor + jnp.sum(expo, axis=2)  6.31 us
    dot_general x17, matrix products, update(): jnp.einsum('hsp,phd->shd', weights, raw_block.reshape(block, heads, HD),...  5.74 us
  transfers between devices with their start and end apart: 6, of which 4 were waited for; matrix products, arithmetic and copies ran while one was open for 7% of the time, Pallas kernels for 0%

commit v1 on v0

--- a/solution.py
+++ b/solution.py
@@ -94,7 +94,9 @@
     )
     values = (stream_f * inverse[:, None] * norm_gain).astype(jnp.bfloat16)
     key_piece = lax.all_gather(attn_keys, "ctx", axis=0, tiled=True)
-    raw_piece = lax.all_gather(values, "ctx", axis=0, tiled=True)
+    raw_piece = jnp.concatenate(
+        lax.all_to_all(jnp.stack([values] * lax.axis_size("ctx")), "ctx", 0, 0), axis=0
+    )
     piece_rows = key_piece.shape[0]
     block = math.gcd(piece_rows, 1536)
 

time: 278 us -> 297 us (1.068)
  the two profiles are of different devices: /device:TPU:443 before, /device:TPU:319 now
where the time goes in v1:
time: 297 us; the launch traced here: 296 us
  waiting for transfers between devices  146 us (49%)
  local copies, waits for them, and re-layouts  37.3 us (13%)
  starting transfers between devices  33.2 us (11%)
  blocking collectives  30.6 us (10%)
  other arithmetic  17.7 us (6%)
  between operations  14.2 us (5%)
  matrix products  12.7 us (4%)
  loops' own time  4.11 us (1%)
    all_gather x1, waiting for transfers between devices, shards(): key_piece = lax.all_gather(attn_keys, 'ctx', axis=0, tiled=True)  143 us
    psum x1, blocking collectives, shards(): row_totals = lax.psum(row_squares, 'tp')  30.6 us
    all_to_all x1, starting transfers between devices, shards(): lax.all_to_all(jnp.stack([values] * lax.axis_size('ctx')), 'ctx', 0, 0)  28.1 us
    dynamic_slice x17, local copies, waits for them, and re-layouts, block_step(): raw_block = lax.dynamic_slice_in_dim(raw_piece, offset, block, 0)  18.3 us
    unnamed x13, local copies, waits for them, and re-layouts  13 us
    dot_general x17, matrix products, update(): jnp.einsum('shd,phd->hsp', query_heads, key_block.reshape(block, heads, H...  6.98 us
    reduce_sum x17, other arithmetic, update(): new_sum = running_sum * factor + jnp.sum(expo, axis=2)  6.31 us
  transfers between devices with their start and end apart: 6, of which 3 were waited for; matrix products, arithmetic and copies ran while one was open for 6% of the time, Pallas kernels for 0%

profile of v1, /device:TPU:319, one launch (start us, length us, event | category | flops | bytes accessed | tf_op | source)
XLA Modules:
  0.0 295.5 jit_solution(7772490203775923589)
XLA Ops:
  8.0 1.3 collective-permute-start.1
  10.0 1.3 collective-permute-start.2
  12.1 1.7 collective-permute-done.2
  13.8 1.5 multiply_convert_fusion
  15.3 1.3 collective-permute-start.3
  17.3 1.3 collective-permute-start
  20.5 8.7 %while.36 = (s32[]{:T(128)}, f32[136,512]{1,0:T(8,128)S(1)}, f32[128,512]{1,0:T(8,128)S(1)}, f32[263,512]{1,0:T(8,128)S(1)}, s32[]{:T(128)}, /*index=5*/s32[]{:T...) while((s32[]{:T(128)}, f32[136,512]{1,0:T(8,128)S(1)}, ...), condition=%wide.region_1.2_spmd.clone, body=%wide.region_0.1_spmd.clone.sunk | while | flops 1183811 | bytes 2835447 | solution.py:41
  29.4 30.6 %psum.7 = f32[136]{0:T(256)S(1)} all-reduce(f32[136]{0:T(256)S(1)} %get-tuple-element.521), channel_id=1, replica_groups=mesh['ctx'=32,'tp'=16] {'tp'}, use_global_device_ids=true, to_apply=%region_3.4 | all-reduce | flops 136 | bytes 1088 | tf_op jit(solution)/shard_map/psum | solution.py:82
  60.2 2.3 stack.2
  62.5 28.1 %all-to-all-start = ((bf16[32,136,512]{2,1,0:T(8,128)(2,1)}), bf16[32,136,512]{2,1,0:T(8,128)(2,1)}, u32[]{:S(2)}, u32[]{:S(2)}) async-start(bf16[32,136,512]{2,1,0:T(8,128)(2,1)} %stack.2), calls=%async_computation | async-start | bytes 8912896 | tf_op jit(solution)/shard_map/all_to_all | solution.py:98
  90.6 143.1 %all-gather.2.cloned.1.call-done = bf16[4352,512]{1,0:T(8,128)(2,1)} async-done(((bf16[136,512]{1,0:T(8,128)(2,1)}), bf16[4352,512]{1,0:T(8,128)(2,1)}) %all-gather.2.cloned.1.call-update) | async-done | bytes 4456464 | tf_op jit(solution)/shard_map/all_gather | solution.py:96
  233.8 6.5 %copy.26 = bf16[4352,512]{0,1:T(8,128)(2,1)} copy(bf16[4352,512]{1,0:T(8,128)(2,1)} %all-gather.2.cloned.1.call-done) | data formatting | bytes 8912896
  240.3 6.5 %copy.28 = bf16[4352,512]{0,1:T(8,128)(2,1)} copy(bf16[4352,512]{1,0:T(8,128)(2,1)} %bitcast.14) | data formatting | bytes 8912896
  246.8 41.1 %while.35 = (s32[]{:T(128)}, f32[4,136]{1,0:T(4,128)S(1)}, f32[4,136]{1,0:T(4,128)S(1)}, f32[136,4,128]{2,0,1:T(8,128)S(1)}, s32[]{:T(128)}, /*index=5*/bf16[435...) while((s32[]{:T(128)}, f32[4,136]{1,0:T(4,128)S(1)}, ...), condition=%wide.region_9.10_spmd.clone, body=%wide.region_4.9_spmd.clone.sunk | while | flops 72732656 | bytes 4118965 | solution.py:141
  246.8 2.4 conditional.3
  246.8 1.1 constant_dynamic-slice_fusion
  249.2 2.4 conditional.3
  249.2 1.1 constant_dynamic-slice_fusion
  251.6 2.4 conditional.3
  251.6 1.1 constant_dynamic-slice_fusion
  254.0 2.4 conditional.3
  254.1 1.1 constant_dynamic-slice_fusion
  256.5 2.4 conditional.3
  256.5 1.1 constant_dynamic-slice_fusion
  258.9 2.4 conditional.3
  258.9 1.1 constant_dynamic-slice_fusion
  261.3 2.4 conditional.3
  261.3 1.1 constant_dynamic-slice_fusion
  263.7 2.4 conditional.3
  263.7 1.1 constant_dynamic-slice_fusion
  266.1 2.4 conditional.3
  266.2 1.1 constant_dynamic-slice_fusion
  268.6 2.4 conditional.3
  268.6 1.1 constant_dynamic-slice_fusion
  271.0 2.4 conditional.3
  271.0 1.1 constant_dynamic-slice_fusion
  273.4 2.4 conditional.3
  273.4 1.1 constant_dynamic-slice_fusion
  275.8 2.4 conditional.3
  275.8 1.1 constant_dynamic-slice_fusion
  278.2 2.4 conditional.3
  278.2 1.1 constant_dynamic-slice_fusion
  280.6 2.4 conditional.3
  280.7 1.1 constant_dynamic-slice_fusion
  283.1 2.4 conditional.3
  283.1 1.1 constant_dynamic-slice_fusion
  285.5 2.4 conditional.3
  285.5 1.1 constant_dynamic-slice_fusion
  (234 shorter events, 33.6 us)
Async XLA Ops:
  7.2 83.4 %copy-start = (bf16[136,512]{1,0:T(8,128)(2,1)S(1)}, bf16[136,512]{1,0:T(8,128)(2,1)}, u32[]{:S(2)}) copy-start(bf16[136,512]{1,0:T(8,128)(2,1)} %param.22) | copy-start | bytes 417796
  7.2 226.6 %all-gather.2.cloned.1.call-start = ((), (), s32[]{:S(2)}) async-start(), calls=%async_computation.1 | async-start | bytes 4595712 | tf_op jit(solution)/shard_map/all_gather | solution.py:96
  8.0 4.2 %collective-permute-start.1 = (bf16[2,512]{1,0:T(2,128)(2,1)S(1)}, bf16[2,512]{1,0:T(2,128)(2,1)S(1)}, u32[]{:S(2)}, u32[]{:S(2)}) collective-permute-start(bf16[2,512]{1,0:T(2,128)(2,1)S(1)} %slice.86), channel_id=1, source_target_pairs={{0,16},{16,32},{32,48},{48,64},{64,80},{80,96},{96,112},{112,128},... | collective-permute-start | bytes 6152 | tf_op jit(solution)/shard_map/ppermute | solution.py:13
  10.0 3.8 %collective-permute-start.2 = (bf16[2,512]{1,0:T(2,128)(2,1)S(1)}, bf16[2,512]{1,0:T(2,128)(2,1)S(1)}, u32[]{:S(2)}, u32[]{:S(2)}) collective-permute-start(bf16[2,512]{1,0:T(2,128)(2,1)S(1)} %slice.92), channel_id=1, source_target_pairs={{0,16},{16,32},{32,48},{48,64},{64,80},{80,96},{96,112},{112,128},... | collective-permute-start | bytes 6152 | tf_op jit(solution)/shard_map/ppermute | solution.py:13
  15.3 5.1 %collective-permute-start.3 = (bf16[127,512]{1,0:T(8,128)(2,1)S(1)}, bf16[127,512]{1,0:T(8,128)(2,1)S(1)}, u32[]{:S(2)}, u32[]{:S(2)}) collective-permute-start(bf16[127,512]{1,0:T(8,128)(2,1)S(1)} %slice.103), channel_id=1, source_target_pairs={{0,16},{16,32},{32,48},{48,64},{64,80},{80,96},{96,112},{112,128},... | collective-permute-start | bytes 390152 | tf_op jit(solution)/shard_map/ppermute | solution.py:13
  17.3 11.9 %collective-permute-start = (bf16[2,512]{1,0:T(2,128)(2,1)S(1)}, bf16[2,512]{1,0:T(2,128)(2,1)S(1)}, u32[]{:S(2)}, u32[]{:S(2)}) collective-permute-start(bf16[2,512]{1,0:T(2,128)(2,1)S(1)} %slice.80), channel_id=1, source_target_pairs={{0,16},{16,32},{32,48},{48,64},{64,80},{80,96},{96,112},{112,128},... | collective-permute-start | bytes 6152 | tf_op jit(solution)/shard_map/ppermute | solution.py:13
  20.5 8.7 %copy-start.2 = (bf16[136,512]{1,0:T(8,128)(2,1)S(1)}, bf16[136,512]{1,0:T(8,128)(2,1)}, u32[]{:S(2)}) copy-start(bf16[136,512]{1,0:T(8,128)(2,1)} %param.17) | copy-start | bytes 417796
  20.5 8.7 %copy-start.3 = (bf16[136,512]{1,0:T(8,128)(2,1)S(1)}, bf16[136,512]{1,0:T(8,128)(2,1)}, u32[]{:S(2)}) copy-start(bf16[136,512]{1,0:T(8,128)(2,1)} %param.15) | copy-start | bytes 417796
  20.5 39.6 %copy-start.4 = (f32[512]{0:T(512)S(1)}, f32[512]{0:T(512)}, u32[]{:S(2)}) copy-start(f32[512]{0:T(512)} %param.21) | copy-start | bytes 6148
  29.4 33.1 %copy-start.1 = (bf16[136,512]{1,0:T(8,128)(2,1)}, bf16[136,512]{1,0:T(8,128)(2,1)S(1)}, u32[]{:S(2)}) copy-start(bf16[136,512]{1,0:T(8,128)(2,1)S(1)} %get-tuple-element.522) | copy-start | bytes 417796
  62.5 177.8 %all-to-all-start = ((bf16[32,136,512]{2,1,0:T(8,128)(2,1)}), bf16[32,136,512]{2,1,0:T(8,128)(2,1)}, u32[]{:S(2)}, u32[]{:S(2)}) async-start(bf16[32,136,512]{2,1,0:T(8,128)(2,1)} %stack.2), calls=%async_computation | async-start | bytes 8912896 | tf_op jit(solution)/shard_map/all_to_all | solution.py:98
Sparse Core Ops, SparseCore 0:
  18.7 214.9 all-gather.1
